TPU v7x, 32 devices: a whole 2x2x4 slice. The times are simulated.
32 devices in a mesh: row: 4 (over x, core), col: 8 (over z, y).
Axes of the slice: x: 2, y: 2, z: 4, core: 2. Of those that a mesh axis runs over, the one named last changes fastest.
Arguments:
- schur: float32 [4096, 4096], P('row', 'col'), may hold values from -6 to 6
- left_rot: float32 [8, 512, 512], P('row', 'col'), may hold values from -1 to 1, as said below
- right_rot: float32 [8, 512, 512], P('col', 'row'), may hold values from -1 to 1, as said below
- left_off: float32 [8, 512, 512], P('row', 'col'), may hold values from -1 to 1, as said below
- right_off: float32 [8, 512, 512], P('col', 'row'), may hold values from -1 to 1, as said below
Outputs:
- updated: float32 [4096, 4096], P('row', 'col')
Inputs may be any that keep to these rules, and one draw needn't show every extreme that they name: `left_rot`: each 512 x 512 block is orthogonal. `right_rot`: each 512 x 512 block is orthogonal. `left_off`: each 512 x 512 block is orthogonal. `right_off`: each 512 x 512 block is orthogonal.
All inputs are finite; a program needn't handle non-finite values.
Results may differ from a plain program's by a relative error of at most 0.00007.
Values sent between devices are 32-bit elements; how exact they have to be, the bound alone decides.
A program may use at most 64 MiB of HBM per device.

v0:
```python
import jax
import jax.numpy as jnp
from jax import lax
from jax.sharding import PartitionSpec as P


def passed_along(x, axis, by):
    size = lax.axis_size(axis)
    return lax.ppermute(x, axis, [(i, (i + by) % size) for i in range(size)])


def padded_2(cells, sides, width):
    for axis, dim in sides:
        count = lax.axis_size(axis)
        head = lax.slice_in_dim(cells, 0, width, axis=dim)
        tail = lax.slice_in_dim(cells, cells.shape[dim] - width, cells.shape[dim], axis=dim)
        cells = jnp.concatenate(
            [
                lax.ppermute(tail, axis, [(i, (i + 1) % count) for i in range(count)]),
                cells,
                lax.ppermute(head, axis, [((i + 1) % count, i) for i in range(count)]),
            ],
            axis=dim,
        )
    return cells


def apply_left(blocks, rotations):
    number = rotations.shape[0]
    window = rotations.shape[1]
    shaped = blocks.reshape(number, window, blocks.shape[1])
    result = jnp.einsum("kab,kac->kbc", rotations, shaped, precision=lax.Precision.HIGHEST)
    return result.reshape(number * window, blocks.shape[1])


def apply_right(blocks, rotations):
    number = rotations.shape[0]
    window = rotations.shape[1]
    shaped = blocks.reshape(blocks.shape[0], number, window)
    result = jnp.einsum("rka,kab->rkb", shaped, rotations, precision=lax.Precision.HIGHEST)
    return result.reshape(blocks.shape[0], number * window)


def body(schur, left_rot, right_rot, left_off, right_off):
    window = left_rot.shape[2]
    half_window = window // 2
    rows_here = schur.shape[0]
    cols_here = schur.shape[1]
    rotations = lax.all_gather(right_rot, "row", axis=1, tiled=True)
    matrix = apply_right(schur, rotations)
    rotations = lax.all_gather(left_rot, "col", axis=1, tiled=True)
    matrix = apply_left(matrix, rotations)
    rotations = lax.all_gather(right_off, "row", axis=1, tiled=True)
    following = passed_along(rotations[0][:, :half_window], "col", -1)
    padded = padded_2(matrix, (("col", 1),), half_window)
    leading = jnp.dot(
        padded[:, :window], rotations[0][:, half_window:], precision=lax.Precision.HIGHEST
    )
    middle = apply_right(padded[:, window:cols_here], rotations[1:])
    trailing = jnp.dot(
        padded[:, cols_here : cols_here + window], following, precision=lax.Precision.HIGHEST
    )
    matrix = jnp.concatenate([leading, middle, trailing], axis=1)
    rotations = lax.all_gather(left_off, "col", axis=1, tiled=True)
    following = passed_along(rotations[0][:, :half_window], "row", -1)
    padded = padded_2(matrix, (("row", 0),), half_window)
    leading = jnp.dot(
        rotations[0][:, half_window:].T, padded[:window], precision=lax.Precision.HIGHEST
    )
    middle = apply_left(padded[window:rows_here], rotations[1:])
    trailing = jnp.dot(
        following.T, padded[rows_here : rows_here + window], precision=lax.Precision.HIGHEST
    )
    return jnp.concatenate([leading, middle, trailing], axis=0)


def solution(mesh):
    return jax.shard_map(
        body,
        mesh=mesh,
        in_specs=(
            P("row", "col"),
            P("row", "col", None),
            P("col", "row", None),
            P("row", "col", None),
            P("col", "row", None),
        ),
        out_specs=P("row", "col"),
        check_vma=False,
    )
```

profile of v0, /device:TPU:1, one launch (start us, length us, event | category | flops | bytes accessed | tf_op | source)
XLA Modules:
  0.0 192.9 jit_solution(4929643086227449214)
XLA Ops:
  9.3 18.8 %all-gather.5.cloned.1.call-done = f32[1,512,512]{2,1,0:T(8,128)} async-done(((f32[1,128,512]{2,1,0:T(8,128)}), f32[1,512,512]{2,1,0:T(8,128)}) %all-gather.5.cloned.1.call-update) | async-done | bytes 1048592 | tf_op jit(solution)/shard_map/all_gather | solution.py:49
  28.1 9.3 %convolution_bitcast_fusion = f32[1024,1,512]{0,2,1:T(8,128)} fusion(f32[1024,512]{1,0:T(8,128)S(1)} %copy-done, f32[1,512,512]{2,1,0:T(8,128)} %all-gather.5.cloned.1.call-done), kind=kOutput, calls=%fused_computation.9 | convolution fusion | flops 3221225472 | bytes 5242880 | tf_op jit(solution)/shard_map/rka,kab->rkb/dot_general | solution.py:40
  37.3 3.0 %copy.7 = f32[1024,1,512]{2,0,1:T(8,128)} copy(f32[1024,1,512]{0,2,1:T(8,128)} %convolution_bitcast_fusion) | data formatting | bytes 4194304 | tf_op jit(solution)/shard_map/reshape;reshape | solution.py:31
  40.3 36.8 %all-gather.7.cloned.1.call-done = f32[2,512,512]{2,1,0:T(8,128)} async-done(((f32[2,64,512]{2,1,0:T(8,128)}), f32[2,512,512]{2,1,0:T(8,128)}) %all-gather.7.cloned.1.call-update) | async-done | bytes 2097168 | tf_op jit(solution)/shard_map/all_gather | solution.py:51
  77.1 5.8 %fusion.17 = f32[2,512,512]{1,2,0:T(8,128)S(1)} fusion(f32[2,512,512]{2,1,0:T(8,128)} %bitcast.31, f32[2,512,512]{2,1,0:T(8,128)} %all-gather.7.cloned.1.call-done), kind=kOutput, calls=%fused_computation.33 | convolution fusion | flops 3221225472 | bytes 6291456 | tf_op jit(solution)/shard_map/kab,kac->kbc/dot_general | solution.py:32
  82.8 1.4 fusion.16
  84.8 3.9 %collective-permute-start.1 = (f32[1024,256]{1,0:T(8,128)}, f32[1024,256]{1,0:T(8,128)}, u32[]{:S(2)}, u32[]{:S(2)}) collective-permute-start(f32[1024,256]{1,0:T(8,128)} %get-tuple-element.8), channel_id=1, source_target_pairs={{1,0},{2,1},{3,2},{4,3},{5,4},{6,5},{7,6},{0,7},{9,8},{10,9},{11,1... | collective-permute-start | bytes 3145736 | tf_op jit(solution)/shard_map/ppermute | solution.py:21
  88.7 7.5 %all-gather.9.cloned.1.call-done = f32[1,512,512]{2,1,0:T(8,128)} async-done(((f32[1,128,512]{2,1,0:T(8,128)}), f32[1,512,512]{2,1,0:T(8,128)}) %all-gather.9.cloned.1.call-update) | async-done | bytes 1048592 | tf_op jit(solution)/shard_map/all_gather | solution.py:53
  96.2 1.1 slice.68
  97.3 4.2 %collective-permute-start.2 = (f32[512,256]{1,0:T(8,128)S(1)}, f32[512,256]{1,0:T(8,128)S(1)}, u32[]{:S(2)}, u32[]{:S(2)}) collective-permute-start(f32[512,256]{1,0:T(8,128)S(1)} %slice.68), channel_id=1, source_target_pairs={{0,7},{1,0},{2,1},{3,2},{4,3},{5,4},{6,5},{7,6},{8,15},{9,8},{10,9... | collective-permute-start | bytes 1572872 | tf_op jit(solution)/shard_map/ppermute | solution.py:9
  101.5 42.8 %collective-permute-done = f32[1024,256]{1,0:T(8,128)} collective-permute-done((f32[1024,256]{1,0:T(8,128)S(1)}, f32[1024,256]{1,0:T(8,128)}, u32[]{:S(2)}, u32[]{:S(2)}) %collective-permute-start) | collective-permute-done | bytes 1048608 | tf_op jit(solution)/shard_map/ppermute | solution.py:19
  144.3 3.6 %fusion.2 = f32[1024,256]{0,1:T(8,128)S(1)} fusion(f32[1024,512]{1,0:T(8,128)} %bitcast.29, f32[1024,256]{1,0:T(8,128)} %collective-permute-done, f32[512,512]{1,0:T(8,128)} %bitcast.33), kind=kOutput, calls=%fused_computation.4 | convolution fusion | flops 1611137024 | bytes 4718592 | tf_op jit(solution)/shard_map/dot_general | solution.py:56
  147.9 6.7 %collective-permute-done.2 = f32[512,256]{1,0:T(8,128)S(1)} collective-permute-done((f32[512,256]{1,0:T(8,128)S(1)}, f32[512,256]{1,0:T(8,128)S(1)}, u32[]{:S(2)}, u32[]{:S(2)}) %collective-permute-start.2) | collective-permute-done | bytes 524320 | tf_op jit(solution)/shard_map/ppermute | solution.py:9
  154.6 3.3 %fusion = f32[1024,256]{0,1:T(8,128)S(1)} fusion(f32[512,256]{1,0:T(8,128)S(1)} %collective-permute-done.2, f32[1024,256]{1,0:T(8,128)} %collective-permute-done.1, f32[1024,512]{1,0:T(8,128)S(1)} %bitcast.30), kind=kOutput, calls=%fused_computation.1 | convolution fusion | flops 1611137024 | bytes 4718592 | tf_op jit(solution)/shard_map/dot_general | solution.py:60
  158.9 1.0 pad_maximum_fusion.14
  159.9 3.7 %collective-permute-start.3 = (f32[256,512]{0,1:T(8,128)}, f32[256,512]{0,1:T(8,128)}, u32[]{:S(2)}, u32[]{:S(2)}) collective-permute-start(f32[256,512]{0,1:T(8,128)} %get-tuple-element.5), channel_id=1, source_target_pairs={{0,8},{8,16},{16,24},{24,0},{1,9},{9,17},{17,25},{25,1},{2,10},{10... | collective-permute-start | bytes 1572872 | tf_op jit(solution)/shard_map/ppermute | solution.py:19
  163.6 4.1 %all-gather.11.cloned.1.call-done = f32[2,512,512]{2,1,0:T(8,128)} async-done(((f32[2,64,512]{2,1,0:T(8,128)}), f32[2,512,512]{2,1,0:T(8,128)}) %all-gather.11.cloned.1.call-update) | async-done | bytes 2097168 | tf_op jit(solution)/shard_map/all_gather | solution.py:64
  167.7 1.4 slice_bitcast_fusion.2
  170.9 1.9 convolution_bitcast_fusion.1
  172.7 2.1 %convolution_bitcast_fusion.3 = f32[256,512]{1,0:T(8,128)S(1)} fusion(f32[256,512]{0,1:T(8,128)} %collective-permute-done.3, f32[1024,256]{0,1:T(8,128)S(1)} %copy-done.4, f32[1024,256]{0,1:T(8,128)S(1)} %fusion.2, f32[512,512]{1,0:T(8,128)S(1)} %slice_bitcast_fusion.2), kind=kOutput, calls=%fused_computation.12 | convolution fusion | flops 805830656 | bytes 3670016 | tf_op jit(solution)/shard_map/dot_general | solution.py:67
  174.9 3.3 %collective-permute-done.5 = f32[512,256]{1,0:T(8,128)S(1)} collective-permute-done((f32[512,256]{1,0:T(8,128)S(1)}, f32[512,256]{1,0:T(8,128)S(1)}, u32[]{:S(2)}, u32[]{:S(2)}) %collective-permute-start.5) | collective-permute-done | bytes 524320 | tf_op jit(solution)/shard_map/ppermute | solution.py:9
  178.2 5.6 %collective-permute-done.4 = f32[256,512]{0,1:T(8,128)S(1)} collective-permute-done((f32[256,512]{0,1:T(8,128)}, f32[256,512]{0,1:T(8,128)S(1)}, u32[]{:S(2)}, u32[]{:S(2)}) %collective-permute-start.4) | collective-permute-done | bytes 524320 | tf_op jit(solution)/shard_map/ppermute | solution.py:21
  183.8 1.1 convolution_bitcast_fusion.2
  184.9 1.5 pad_maximum_fusion.4
  (26 shorter events, 6.0 us)
Async XLA Ops:
  6.5 21.5 %copy-start = (f32[1024,512]{1,0:T(8,128)S(1)}, f32[1024,512]{1,0:T(8,128)}, u32[]{:S(2)}) copy-start(f32[1024,512]{1,0:T(8,128)} %param.5) | copy-start | bytes 6291460
  6.5 21.5 %all-gather.5.cloned.1.call-start = ((), (), s32[]{:S(2)}) async-start(), calls=%async_computation | async-start | bytes 1310720 | tf_op jit(solution)/shard_map/all_gather | solution.py:49
  7.3 69.8 %all-gather.7.cloned.1.call-start = ((), (), s32[]{:S(2)}) async-start(), calls=%async_computation.1 | async-start | bytes 2359296 | tf_op jit(solution)/shard_map/all_gather | solution.py:51
  8.0 88.2 %all-gather.9.cloned.1.call-start = ((), (), s32[]{:S(2)}) async-start(), calls=%async_computation.2 | async-start | bytes 1310720 | tf_op jit(solution)/shard_map/all_gather | solution.py:53
  8.7 159.0 %all-gather.11.cloned.1.call-start = ((), (), s32[]{:S(2)}) async-start(), calls=%async_computation.3 | async-start | bytes 2359296 | tf_op jit(solution)/shard_map/all_gather | solution.py:64
  82.8 1.7 copy-start.1
  84.5 59.8 %collective-permute-start = (f32[1024,256]{1,0:T(8,128)S(1)}, f32[1024,256]{1,0:T(8,128)}, u32[]{:S(2)}, u32[]{:S(2)}) collective-permute-start(f32[1024,256]{1,0:T(8,128)S(1)} %get-tuple-element.7), channel_id=1, source_target_pairs={{0,1},{1,2},{2,3},{3,4},{4,5},{5,6},{6,7},{7,0},{8,9},{9,10},{10,1... | collective-permute-start | bytes 3145736 | tf_op jit(solution)/shard_map/ppermute | solution.py:19
  84.8 69.9 %collective-permute-start.1 = (f32[1024,256]{1,0:T(8,128)}, f32[1024,256]{1,0:T(8,128)}, u32[]{:S(2)}, u32[]{:S(2)}) collective-permute-start(f32[1024,256]{1,0:T(8,128)} %get-tuple-element.8), channel_id=1, source_target_pairs={{1,0},{2,1},{3,2},{4,3},{5,4},{6,5},{7,6},{0,7},{9,8},{10,9},{11,1... | collective-permute-start | bytes 3145736 | tf_op jit(solution)/shard_map/ppermute | solution.py:21
  97.3 57.4 %copy-start.2 = (f32[2,512,512]{1,2,0:T(8,128)S(1)}, f32[2,512,512]{1,2,0:T(8,128)}, u32[]{:S(2)}) copy-start(f32[2,512,512]{1,2,0:T(8,128)} %copy-done.1) | copy-start | bytes 6291460
  97.3 57.3 %collective-permute-start.2 = (f32[512,256]{1,0:T(8,128)S(1)}, f32[512,256]{1,0:T(8,128)S(1)}, u32[]{:S(2)}, u32[]{:S(2)}) collective-permute-start(f32[512,256]{1,0:T(8,128)S(1)} %slice.68), channel_id=1, source_target_pairs={{0,7},{1,0},{2,1},{3,2},{4,3},{5,4},{6,5},{7,6},{8,15},{9,8},{10,9... | collective-permute-start | bytes 1572872 | tf_op jit(solution)/shard_map/ppermute | solution.py:9
  157.9 1.0 copy-start.3
  159.9 12.8 %collective-permute-start.3 = (f32[256,512]{0,1:T(8,128)}, f32[256,512]{0,1:T(8,128)}, u32[]{:S(2)}, u32[]{:S(2)}) collective-permute-start(f32[256,512]{0,1:T(8,128)} %get-tuple-element.5), channel_id=1, source_target_pairs={{0,8},{8,16},{16,24},{24,0},{1,9},{9,17},{17,25},{25,1},{2,10},{10... | collective-permute-start | bytes 1572872 | tf_op jit(solution)/shard_map/ppermute | solution.py:19
  167.7 3.1 %copy-start.4 = (f32[1024,256]{0,1:T(8,128)S(1)}, f32[1024,256]{0,1:T(8,128)}, u32[]{:S(2)}) copy-start(f32[1024,256]{0,1:T(8,128)} %copy-done.3) | copy-start | bytes 3145732
  167.7 3.1 %copy-start.5 = (f32[2,512,512]{2,1,0:T(8,128)S(1)}, f32[2,512,512]{2,1,0:T(8,128)}, u32[]{:S(2)}) copy-start(f32[2,512,512]{2,1,0:T(8,128)} %all-gather.11.cloned.1.call-done) | copy-start | bytes 6291460
  169.2 9.0 %collective-permute-start.5 = (f32[512,256]{1,0:T(8,128)S(1)}, f32[512,256]{1,0:T(8,128)S(1)}, u32[]{:S(2)}, u32[]{:S(2)}) collective-permute-start(f32[512,256]{1,0:T(8,128)S(1)} %slice.74), channel_id=1, source_target_pairs={{0,24},{8,0},{16,8},{24,16},{1,25},{9,1},{17,9},{25,17},{2,26},{10... | collective-permute-start | bytes 1572872 | tf_op jit(solution)/shard_map/ppermute | solution.py:9
  170.2 13.6 %collective-permute-start.4 = (f32[256,512]{0,1:T(8,128)}, f32[256,512]{0,1:T(8,128)S(1)}, u32[]{:S(2)}, u32[]{:S(2)}) collective-permute-start(f32[256,512]{0,1:T(8,128)} %get-tuple-element.6), channel_id=1, source_target_pairs={{8,0},{16,8},{24,16},{0,24},{9,1},{17,9},{25,17},{1,25},{10,2},{18... | collective-permute-start | bytes 1572872 | tf_op jit(solution)/shard_map/ppermute | solution.py:21
Sparse Core Ops, SparseCore 0:
  8.9 19.1 all-gather.4
  30.3 46.7 all-gather.6
  78.6 17.5 all-gather.8
  98.2 69.4 all-gather.10
where the time goes:
time: 193 us
  waiting for transfers between devices  128 us (66%)
  matrix products  27.1 us (14%)
  starting transfers between devices  13.8 us (7%)
  between operations  13.2 us (7%)
  local copies, waits for them, and re-layouts  8.15 us (4%)
  other arithmetic  2.53 us (1%)
    ppermute x2, waiting for transfers between devices, padded_2(): lax.ppermute(tail, axis, [(i, (i + 1) % count) for i in range(count)])  42.8 us
    all_gather x1, waiting for transfers between devices, body(): rotations = lax.all_gather(left_rot, 'col', axis=1, tiled=True)  36.8 us
    all_gather x1, waiting for transfers between devices, body(): rotations = lax.all_gather(right_rot, 'row', axis=1, tiled=True)  18.8 us
    ppermute x2, waiting for transfers between devices, passed_along(): return lax.ppermute(x, axis, [(i, (i + by) % size) for i in range(size)])  9.97 us
    dot_general x1, matrix products, apply_right(): jnp.einsum('rka,kab->rkb', shaped, rotations, precision=lax.Precision.HIG...  9.25 us
    dot_general x2, matrix products, apply_left(): jnp.einsum('kab,kac->kbc', rotations, shaped, precision=lax.Precision.HIG...  7.62 us
    all_gather x1, waiting for transfers between devices, body(): rotations = lax.all_gather(right_off, 'row', axis=1, tiled=True)  7.54 us
    ppermute x2, waiting for transfers between devices, padded_2(): lax.ppermute(head, axis, [((i + 1) % count, i) for i in range(count)])  5.62 us
  transfers between devices with their start and end apart: 10, of which 8 were waited for; matrix products, arithmetic and copies ran while one was open for 18% of the time, Pallas kernels for 0%

commit v1 on v0

--- a/solution.py
+++ b/solution.py
@@ -46,7 +46,9 @@
     half_window = window // 2
     rows_here = schur.shape[0]
     cols_here = schur.shape[1]
-    rotations = lax.all_gather(right_rot, "row", axis=1, tiled=True)
+    rotations = jnp.concatenate(
+        lax.all_to_all(jnp.stack([right_rot] * lax.axis_size("row")), "row", 0, 0), axis=1
+    )
     matrix = apply_right(schur, rotations)
     rotations = lax.all_gather(left_rot, "col", axis=1, tiled=True)
     matrix = apply_left(matrix, rotations)

time: 193 us -> 175 us (0.907)
  waiting for transfers between devices: 128 us -> 92.5 us
  blocking collectives: 0 us -> 17.4 us
    all_gather x1 -> x0, waiting for transfers between devices: 18.8 us -> none  [body(): rotations = lax.all_gather(right_rot, 'row', axis=1, tiled=True)]
    all_to_all x0 -> x1, blocking collectives: none -> 17.4 us  [body(): lax.all_to_all(jnp.stack([right_rot] * lax.axis_size('row')), 'row', 0, 0)]
    all_gather x1, waiting for transfers between devices: 36.8 us -> 20.4 us  [body(): rotations = lax.all_gather(left_rot, 'col', axis=1, tiled=True)]
  transfers between devices with their start and end apart: 10 -> 9, of which waited for: 8 -> 7; matrix products, arithmetic and copies ran while one was open for 18% -> 19% of each run, Pallas kernels for 0% -> 0%
where the time goes in v1:
time: 175 us
  waiting for transfers between devices  92.5 us (53%)
  matrix products  26 us (15%)
  blocking collectives  17.4 us (10%)
  starting transfers between devices  13.8 us (8%)
  between operations  13.2 us (8%)
  local copies, waits for them, and re-layouts  9.17 us (5%)
  other arithmetic  2.53 us (1%)
    ppermute x2, waiting for transfers between devices, padded_2(): lax.ppermute(tail, axis, [(i, (i + 1) % count) for i in range(count)])  42.8 us
    all_gather x1, waiting for transfers between devices, body(): rotations = lax.all_gather(left_rot, 'col', axis=1, tiled=True)  20.4 us
    all_to_all x1, blocking collectives, body(): lax.all_to_all(jnp.stack([right_rot] * lax.axis_size('row')), 'row', 0, 0)  17.4 us
    ppermute x2, waiting for transfers between devices, passed_along(): return lax.ppermute(x, axis, [(i, (i + by) % size) for i in range(size)])  9.99 us
    dot_general x1, matrix products, apply_right(): jnp.einsum('rka,kab->rkb', shaped, rotations, precision=lax.Precision.HIG...  8.21 us
    dot_general x2, matrix products, apply_left(): jnp.einsum('kab,kac->kbc', rotations, shaped, precision=lax.Precision.HIG...  7.62 us
    all_gather x1, waiting for transfers between devices, body(): rotations = lax.all_gather(right_off, 'row', axis=1, tiled=True)  7.54 us
    ppermute x2, waiting for transfers between devices, padded_2(): lax.ppermute(head, axis, [((i + 1) % count, i) for i in range(count)])  5.62 us
  transfers between devices with their start and end apart: 9, of which 7 were waited for; matrix products, arithmetic and copies ran while one was open for 19% of the time, Pallas kernels for 0%

profile of v1, /device:TPU:1, one launch (start us, length us, event | category | flops | bytes accessed | tf_op | source)
XLA Modules:
  0.0 174.6 jit_solution(11007314293581148346)
XLA Ops:
  8.7 1.1 stack.2
  9.8 17.4 %all_to_all.5 = f32[4,1,128,512]{3,2,1,0:T(8,128)S(1)} all-to-all(f32[4,1,128,512]{3,2,1,0:T(8,128)S(1)} %stack.2), channel_id=1, replica_groups=mesh['row'=4,'col'=8] {'row'}, dimensions={0} | all-to-all | bytes 2097152 | tf_op jit(solution)/shard_map/all_to_all | solution.py:50
  27.3 8.2 %convolution_bitcast_fusion = f32[1024,1,512]{0,2,1:T(8,128)} fusion(f32[512,512]{1,0:T(8,128)S(1)} %bitcast.32, f32[1024,512]{1,0:T(8,128)S(1)} %copy-done), kind=kOutput, calls=%fused_computation.9 | convolution fusion | flops 3221225472 | bytes 5242880 | tf_op jit(solution)/shard_map/rka,kab->rkb/dot_general | solution.py:40
  35.5 2.9 %copy.7 = f32[1024,1,512]{2,0,1:T(8,128)} copy(f32[1024,1,512]{0,2,1:T(8,128)} %convolution_bitcast_fusion) | data formatting | bytes 4194304 | tf_op jit(solution)/shard_map/reshape;reshape | solution.py:31
  38.4 20.4 %all-gather.4.cloned.1.call-done = f32[2,512,512]{2,1,0:T(8,128)} async-done(((f32[2,64,512]{2,1,0:T(8,128)}), f32[2,512,512]{2,1,0:T(8,128)}) %all-gather.4.cloned.1.call-update) | async-done | bytes 2097168 | tf_op jit(solution)/shard_map/all_gather | solution.py:53
  58.8 5.8 %fusion.16 = f32[2,512,512]{1,2,0:T(8,128)S(1)} fusion(f32[2,512,512]{2,1,0:T(8,128)} %bitcast.31, f32[2,512,512]{2,1,0:T(8,128)} %all-gather.4.cloned.1.call-done), kind=kOutput, calls=%fused_computation.32 | convolution fusion | flops 3221225472 | bytes 6291456 | tf_op jit(solution)/shard_map/kab,kac->kbc/dot_general | solution.py:32
  64.5 1.3 fusion.15
  66.5 3.9 %collective-permute-start.1 = (f32[1024,256]{1,0:T(8,128)}, f32[1024,256]{1,0:T(8,128)}, u32[]{:S(2)}, u32[]{:S(2)}) collective-permute-start(f32[1024,256]{1,0:T(8,128)} %get-tuple-element.8), channel_id=1, source_target_pairs={{1,0},{2,1},{3,2},{4,3},{5,4},{6,5},{7,6},{0,7},{9,8},{10,9},{11,1... | collective-permute-start | bytes 3145736 | tf_op jit(solution)/shard_map/ppermute | solution.py:21
  70.4 7.5 %all-gather.6.cloned.1.call-done = f32[1,512,512]{2,1,0:T(8,128)} async-done(((f32[1,128,512]{2,1,0:T(8,128)}), f32[1,512,512]{2,1,0:T(8,128)}) %all-gather.6.cloned.1.call-update) | async-done | bytes 1048592 | tf_op jit(solution)/shard_map/all_gather | solution.py:55
  77.9 1.1 slice.68
  79.0 4.2 %collective-permute-start.2 = (f32[512,256]{1,0:T(8,128)S(1)}, f32[512,256]{1,0:T(8,128)S(1)}, u32[]{:S(2)}, u32[]{:S(2)}) collective-permute-start(f32[512,256]{1,0:T(8,128)S(1)} %slice.68), channel_id=1, source_target_pairs={{0,7},{1,0},{2,1},{3,2},{4,3},{5,4},{6,5},{7,6},{8,15},{9,8},{10,9... | collective-permute-start | bytes 1572872 | tf_op jit(solution)/shard_map/ppermute | solution.py:9
  83.2 42.8 %collective-permute-done = f32[1024,256]{1,0:T(8,128)} collective-permute-done((f32[1024,256]{1,0:T(8,128)S(1)}, f32[1024,256]{1,0:T(8,128)}, u32[]{:S(2)}, u32[]{:S(2)}) %collective-permute-start) | collective-permute-done | bytes 1048608 | tf_op jit(solution)/shard_map/ppermute | solution.py:19
  126.0 3.6 %fusion.2 = f32[1024,256]{0,1:T(8,128)S(1)} fusion(f32[1024,512]{1,0:T(8,128)} %bitcast.29, f32[1024,256]{1,0:T(8,128)} %collective-permute-done, f32[512,512]{1,0:T(8,128)} %bitcast.34), kind=kOutput, calls=%fused_computation.4 | convolution fusion | flops 1611137024 | bytes 4718592 | tf_op jit(solution)/shard_map/dot_general | solution.py:58
  129.6 6.7 %collective-permute-done.2 = f32[512,256]{1,0:T(8,128)S(1)} collective-permute-done((f32[512,256]{1,0:T(8,128)S(1)}, f32[512,256]{1,0:T(8,128)S(1)}, u32[]{:S(2)}, u32[]{:S(2)}) %collective-permute-start.2) | collective-permute-done | bytes 524320 | tf_op jit(solution)/shard_map/ppermute | solution.py:9
  136.3 3.3 %fusion = f32[1024,256]{0,1:T(8,128)S(1)} fusion(f32[512,256]{1,0:T(8,128)S(1)} %collective-permute-done.2, f32[1024,256]{1,0:T(8,128)} %collective-permute-done.1, f32[1024,512]{1,0:T(8,128)S(1)} %bitcast.30), kind=kOutput, calls=%fused_computation.1 | convolution fusion | flops 1611137024 | bytes 4718592 | tf_op jit(solution)/shard_map/dot_general | solution.py:62
  141.6 3.7 %collective-permute-start.3 = (f32[256,512]{0,1:T(8,128)}, f32[256,512]{0,1:T(8,128)}, u32[]{:S(2)}, u32[]{:S(2)}) collective-permute-start(f32[256,512]{0,1:T(8,128)} %get-tuple-element.5), channel_id=1, source_target_pairs={{0,8},{8,16},{16,24},{24,0},{1,9},{9,17},{17,25},{25,1},{2,10},{10... | collective-permute-start | bytes 1572872 | tf_op jit(solution)/shard_map/ppermute | solution.py:19
  145.4 4.1 %all-gather.8.cloned.1.call-done = f32[2,512,512]{2,1,0:T(8,128)} async-done(((f32[2,64,512]{2,1,0:T(8,128)}), f32[2,512,512]{2,1,0:T(8,128)}) %all-gather.8.cloned.1.call-update) | async-done | bytes 2097168 | tf_op jit(solution)/shard_map/all_gather | solution.py:66
  149.4 1.4 slice_bitcast_fusion.2
  152.6 1.9 %convolution_bitcast_fusion.1 = f32[512,512]{1,0:T(8,128)S(1)} fusion(f32[1024,256]{0,1:T(8,128)S(1)} %fusion.2, f32[1024,256]{0,1:T(8,128)S(1)} %copy-done.4, f32[2,512,512]{2,1,0:T(8,128)S(1)} %copy-done.5), kind=kOutput, calls=%fused_computation.10 | convolution fusion | flops 1610874880 | bytes 4194304 | tf_op jit(solution)/shard_map/kab,kac->kbc/dot_general | solution.py:32
  154.4 2.1 %convolution_bitcast_fusion.3 = f32[256,512]{1,0:T(8,128)S(1)} fusion(f32[256,512]{0,1:T(8,128)} %collective-permute-done.3, f32[1024,256]{0,1:T(8,128)S(1)} %copy-done.4, f32[1024,256]{0,1:T(8,128)S(1)} %fusion.2, f32[512,512]{1,0:T(8,128)S(1)} %slice_bitcast_fusion.2), kind=kOutput, calls=%fused_computation.12 | convolution fusion | flops 805830656 | bytes 3670016 | tf_op jit(solution)/shard_map/dot_general | solution.py:69
  156.6 3.3 %collective-permute-done.5 = f32[512,256]{1,0:T(8,128)S(1)} collective-permute-done((f32[512,256]{1,0:T(8,128)S(1)}, f32[512,256]{1,0:T(8,128)S(1)}, u32[]{:S(2)}, u32[]{:S(2)}) %collective-permute-start.5) | collective-permute-done | bytes 524320 | tf_op jit(solution)/shard_map/ppermute | solution.py:9
  159.9 5.6 %collective-permute-done.4 = f32[256,512]{0,1:T(8,128)S(1)} collective-permute-done((f32[256,512]{0,1:T(8,128)}, f32[256,512]{0,1:T(8,128)S(1)}, u32[]{:S(2)}, u32[]{:S(2)}) %collective-permute-start.4) | collective-permute-done | bytes 524320 | tf_op jit(solution)/shard_map/ppermute | solution.py:21
  165.5 1.1 convolution_bitcast_fusion.2
  166.6 1.5 pad_maximum_fusion.4
  (25 shorter events, 6.4 us)
Async XLA Ops:
  6.5 20.7 %copy-start = (f32[1024,512]{1,0:T(8,128)S(1)}, f32[1024,512]{1,0:T(8,128)}, u32[]{:S(2)}) copy-start(f32[1024,512]{1,0:T(8,128)} %param.5) | copy-start | bytes 6291460
  6.5 52.2 %all-gather.4.cloned.1.call-start = ((), (), s32[]{:S(2)}) async-start(), calls=%async_computation.1 | async-start | bytes 2359296 | tf_op jit(solution)/shard_map/all_gather | solution.py:53
  7.3 70.6 %all-gather.6.cloned.1.call-start = ((), (), s32[]{:S(2)}) async-start(), calls=%async_computation.2 | async-start | bytes 1310720 | tf_op jit(solution)/shard_map/all_gather | solution.py:55
  8.0 141.4 %all-gather.8.cloned.1.call-start = ((), (), s32[]{:S(2)}) async-start(), calls=%async_computation.3 | async-start | bytes 2359296 | tf_op jit(solution)/shard_map/all_gather | solution.py:66
  64.5 1.7 copy-start.1
  66.2 59.8 %collective-permute-start = (f32[1024,256]{1,0:T(8,128)S(1)}, f32[1024,256]{1,0:T(8,128)}, u32[]{:S(2)}, u32[]{:S(2)}) collective-permute-start(f32[1024,256]{1,0:T(8,128)S(1)} %get-tuple-element.7), channel_id=1, source_target_pairs={{0,1},{1,2},{2,3},{3,4},{4,5},{5,6},{6,7},{7,0},{8,9},{9,10},{10,1... | collective-permute-start | bytes 3145736 | tf_op jit(solution)/shard_map/ppermute | solution.py:19
  66.5 69.9 %collective-permute-start.1 = (f32[1024,256]{1,0:T(8,128)}, f32[1024,256]{1,0:T(8,128)}, u32[]{:S(2)}, u32[]{:S(2)}) collective-permute-start(f32[1024,256]{1,0:T(8,128)} %get-tuple-element.8), channel_id=1, source_target_pairs={{1,0},{2,1},{3,2},{4,3},{5,4},{6,5},{7,6},{0,7},{9,8},{10,9},{11,1... | collective-permute-start | bytes 3145736 | tf_op jit(solution)/shard_map/ppermute | solution.py:21
  79.0 57.4 %copy-start.2 = (f32[2,512,512]{1,2,0:T(8,128)S(1)}, f32[2,512,512]{1,2,0:T(8,128)}, u32[]{:S(2)}) copy-start(f32[2,512,512]{1,2,0:T(8,128)} %copy-done.1) | copy-start | bytes 6291460
  79.0 57.3 %collective-permute-start.2 = (f32[512,256]{1,0:T(8,128)S(1)}, f32[512,256]{1,0:T(8,128)S(1)}, u32[]{:S(2)}, u32[]{:S(2)}) collective-permute-start(f32[512,256]{1,0:T(8,128)S(1)} %slice.68), channel_id=1, source_target_pairs={{0,7},{1,0},{2,1},{3,2},{4,3},{5,4},{6,5},{7,6},{8,15},{9,8},{10,9... | collective-permute-start | bytes 1572872 | tf_op jit(solution)/shard_map/ppermute | solution.py:9
  139.6 1.0 copy-start.3
  141.6 12.8 %collective-permute-start.3 = (f32[256,512]{0,1:T(8,128)}, f32[256,512]{0,1:T(8,128)}, u32[]{:S(2)}, u32[]{:S(2)}) collective-permute-start(f32[256,512]{0,1:T(8,128)} %get-tuple-element.5), channel_id=1, source_target_pairs={{0,8},{8,16},{16,24},{24,0},{1,9},{9,17},{17,25},{25,1},{2,10},{10... | collective-permute-start | bytes 1572872 | tf_op jit(solution)/shard_map/ppermute | solution.py:19
  149.4 3.1 %copy-start.4 = (f32[1024,256]{0,1:T(8,128)S(1)}, f32[1024,256]{0,1:T(8,128)}, u32[]{:S(2)}) copy-start(f32[1024,256]{0,1:T(8,128)} %copy-done.3) | copy-start | bytes 3145732
  149.4 3.1 %copy-start.5 = (f32[2,512,512]{2,1,0:T(8,128)S(1)}, f32[2,512,512]{2,1,0:T(8,128)}, u32[]{:S(2)}) copy-start(f32[2,512,512]{2,1,0:T(8,128)} %all-gather.8.cloned.1.call-done) | copy-start | bytes 6291460
  150.9 9.0 %collective-permute-start.5 = (f32[512,256]{1,0:T(8,128)S(1)}, f32[512,256]{1,0:T(8,128)S(1)}, u32[]{:S(2)}, u32[]{:S(2)}) collective-permute-start(f32[512,256]{1,0:T(8,128)S(1)} %slice.74), channel_id=1, source_target_pairs={{0,24},{8,0},{16,8},{24,16},{1,25},{9,1},{17,9},{25,17},{2,26},{10... | collective-permute-start | bytes 1572872 | tf_op jit(solution)/shard_map/ppermute | solution.py:9
  151.9 13.6 %collective-permute-start.4 = (f32[256,512]{0,1:T(8,128)}, f32[256,512]{0,1:T(8,128)S(1)}, u32[]{:S(2)}, u32[]{:S(2)}) collective-permute-start(f32[256,512]{0,1:T(8,128)} %get-tuple-element.6), channel_id=1, source_target_pairs={{8,0},{16,8},{24,16},{0,24},{9,1},{17,9},{25,17},{1,25},{10,2},{18... | collective-permute-start | bytes 1572872 | tf_op jit(solution)/shard_map/ppermute | solution.py:21
Sparse Core Ops, SparseCore 0:
  9.5 49.2 all-gather.3
  60.3 17.5 all-gather.5
  80.1 69.2 all-gather.7
